TPU v7x, 32 devices: a whole 2x2x4 slice. The times are simulated.
32 devices in a mesh: expert: 16 (over z, y, x), etp: 2 (over core).
Axes of the slice: x: 2, y: 2, z: 4, core: 2. Of those that a mesh axis runs over, the one named last changes fastest.
Arguments:
- grad_out: bfloat16 [2048, 3584], P('expert', 'etp'), may hold values from -6 to 6
- combine: bfloat16 [2048, 8], P('expert'), may hold values from 0.099609375 to 2.5
- expert_ids: int32 [2048, 8], P('expert'), may hold values from 0 to 31, all different within a row; in each aligned block of 128 rows (0 to 127, 128 to 255, ...) at most 64 rows name the same one
- saved_gate: bfloat16 [1024, 32, 1024], P(None, 'expert', 'etp'), may hold values from -6 to 6
- saved_up: bfloat16 [1024, 32, 1024], P(None, 'expert', 'etp'), may hold values from -1.5 to 1.5
- gate_weight: bfloat16 [32, 3584, 1024], P('expert', None, 'etp'), may hold values from -0.09375 to 0.09375
- up_weight: bfloat16 [32, 3584, 1024], P('expert', None, 'etp'), may hold values from -0.09375 to 0.09375
- down_weight: bfloat16 [32, 1024, 3584], P('expert', 'etp'), may hold values from -0.09375 to 0.09375
Outputs:
- grad_tokens: bfloat16 [2048, 3584], P('expert', 'etp')
- grad_combine: bfloat16 [2048, 8], P('expert')
Inputs may be any that keep to these rules, and one draw needn't show every extreme that they name: `expert_ids`: each token names 8 different experts. Among the 128 tokens of one block (one index of expert), at most 64 name any one expert, and some blocks reach that bound.
All inputs are finite; a program needn't handle non-finite values.
Results may differ from a plain program's by a relative error of at most 0.012.
Values may be sent and summed in bfloat16 or wider, within the bound.
A program may use at most 192 MiB of HBM per device.

v0:
```python
import jax
import jax.numpy as jnp
from jax import lax
from jax.sharding import PartitionSpec as P


def on_device(
    grad_out, combine, expert_ids, saved_gate, saved_up, gate_weight, up_weight, down_weight
):
    groups = lax.axis_size("expert")
    per_group = gate_weight.shape[0]
    tokens = grad_out.shape[0]
    capacity = saved_gate.shape[0] // groups
    hidden = saved_gate.shape[2]
    experts = groups * per_group
    chosen = expert_ids[:, :, None] == jnp.arange(experts, dtype=jnp.int32)[None, None, :]
    weights = jnp.sum(jnp.where(chosen, combine[:, :, None].astype(jnp.float32), 0.0), axis=1)
    weights = weights.astype(jnp.bfloat16).reshape(tokens, groups, per_group)
    weights = lax.all_to_all(
        weights.transpose(1, 2, 0), "expert", split_axis=0, concat_axis=0, tiled=True
    )
    rows = lax.all_gather(grad_out, "expert", axis=0, tiled=True)
    rows = lax.all_gather(rows, "etp", axis=1, tiled=True)
    rows = rows.reshape(groups, tokens, -1)
    named = (weights > 0).astype(jnp.float32)
    position = jnp.cumsum(named, axis=2) - named
    slot = jnp.where(named > 0, position, -1.0)
    select = slot[:, :, None, :] == jnp.arange(capacity, dtype=jnp.float32)[None, None, :, None]
    scale = jnp.sum(jnp.where(select, weights[:, :, None, :].astype(jnp.float32), 0.0), axis=3)
    scale = scale.transpose(1, 0, 2)[..., None]
    select = select.astype(jnp.bfloat16)
    slot_rows = jnp.einsum("blct,btd->lbcd", select, rows, preferred_element_type=jnp.bfloat16)
    grad_hidden = jnp.einsum(
        "lbcd,lfd->lbcf", slot_rows, down_weight, preferred_element_type=jnp.float32
    )
    gate_value = saved_gate.reshape(groups, capacity, per_group, hidden).transpose(2, 0, 1, 3)
    up_value = saved_up.reshape(groups, capacity, per_group, hidden).transpose(2, 0, 1, 3)
    gate_value = gate_value.astype(jnp.float32)
    up_value = up_value.astype(jnp.float32)
    gate_sigmoid = jax.nn.sigmoid(gate_value)
    activated = gate_value * gate_sigmoid
    weight_part = jnp.sum(grad_hidden * activated * up_value, axis=3)
    scaled = scale * grad_hidden
    grad_gate = (
        scaled * up_value * gate_sigmoid * (1.0 + gate_value * (1.0 - gate_sigmoid))
    ).astype(jnp.bfloat16)
    grad_up = (scaled * activated).astype(jnp.bfloat16)
    weight_tok = jnp.einsum(
        "blct,lbc->blt",
        select,
        weight_part.astype(jnp.bfloat16),
        preferred_element_type=jnp.float32,
    ).astype(jnp.bfloat16)
    weight_tok = lax.psum(weight_tok, "etp")
    weight_tok = lax.all_to_all(weight_tok, "expert", split_axis=0, concat_axis=0, tiled=True)
    weight_tok = weight_tok.transpose(2, 0, 1).reshape(tokens, 1, experts)
    grad_combine = jnp.sum(jnp.where(chosen, weight_tok.astype(jnp.float32), 0.0), axis=2).astype(
        jnp.bfloat16
    )
    partial = jnp.einsum(
        "lbcf,ldf->lbcd", grad_gate, gate_weight, preferred_element_type=jnp.float32
    )
    partial = partial + jnp.einsum(
        "lbcf,ldf->lbcd", grad_up, up_weight, preferred_element_type=jnp.float32
    )
    partial = jnp.einsum(
        "blct,lbcd->btd", select, partial.astype(jnp.bfloat16), preferred_element_type=jnp.float32
    ).astype(jnp.bfloat16)
    partial = partial.reshape(groups * tokens, -1)
    partial = lax.psum_scatter(partial, "etp", scatter_dimension=1, tiled=True)
    grad_tokens = lax.psum_scatter(partial, "expert", scatter_dimension=0, tiled=True)
    return (grad_tokens, grad_combine)


def solution(mesh):
    in_specs = (
        P("expert", "etp"),
        P("expert", None),
        P("expert", None),
        P(None, "expert", "etp"),
        P(None, "expert", "etp"),
        P("expert", None, "etp"),
        P("expert", None, "etp"),
        P("expert", "etp", None),
    )
    out_specs = (P("expert", "etp"), P("expert", None))
    return jax.shard_map(
        on_device, mesh=mesh, in_specs=in_specs, out_specs=out_specs, check_vma=False
    )
```

profile of v0, /device:TPU:10, one launch (start us, length us, event | category | flops | bytes accessed | tf_op | source)
XLA Modules:
  0.0 413.3 jit_solution(12846402701796683711)
XLA Ops:
  7.2 0.0 copy-start.3
  7.2 0.0 copy-start.2
  7.2 0.0 copy-start
  7.2 0.0 all-gather.3.cloned.1.call-start
  7.2 0.7 all-gather.3.cloned.1.call-update
  7.9 0.0 all-gather.5.cloned.1.call-start
  8.0 106.1 %all-gather.3.cloned.1.call-done = bf16[2048,1792]{1,0:T(8,128)(2,1)} async-done(((bf16[128,1792]{1,0:T(8,128)(2,1)}), bf16[2048,1792]{1,0:T(8,128)(2,1)}) %all-gather.3.cloned.1.call-update) | async-done | bytes 7340048 | tf_op jit(solution)/shard_map/all_gather | solution.py:22
  114.0 0.0 all-gather.5.cloned.1.call-update
  114.1 0.0 copy-done.3
  114.1 0.0 copy-done.2
  114.1 0.6 select_reduce_fusion.2
  114.7 5.0 %all-to-all-start = ((bf16[16,2,128]{2,1,0:T(2,128)(2,1)}), bf16[16,2,128]{2,1,0:T(2,128)(2,1)S(1)}, u32[]{:S(2)}, u32[]{:S(2)}) async-start(bf16[16,2,128]{2,1,0:T(2,128)(2,1)} %bitcast.1), calls=%async_computation | async-start | bytes 16384 | tf_op jit(solution)/shard_map/all_to_all | solution.py:19
  119.7 0.0 reduce-scatter.3.cloned.1.call-start
  119.8 0.0 copy-done
  119.8 3.1 copy.40
  122.9 0.0 copy-start.1
  122.9 4.2 %convert_element_type.97 = f32[1024,2,512]{2,1,0:T(2,128)} convert(bf16[1024,2,512]{2,1,0:T(2,128)(2,1)S(1)} %copy-done) | non-fusion elementwise | flops 1048576 | bytes 6291456 | tf_op jit(solution)/shard_map/convert_element_type | solution.py:38
  127.1 0.0 copy-done.1
  127.1 2.9 copy.39
  130.0 3.9 convert_element_type.96
  133.9 0.0 all-to-all-done
  133.9 0.8 reduce_window_sum.11
  134.7 0.4 select_reduce_fusion
  135.1 6.8 %all-gather.5.cloned.1.call-done = bf16[2048,3584]{1,0:T(8,128)(2,1)} async-done(((bf16[2048,1792]{1,0:T(8,128)(2,1)}), bf16[2048,3584]{1,0:T(8,128)(2,1)}) %all-gather.5.cloned.1.call-update) | async-done | bytes 14680080 | tf_op jit(solution)/shard_map/all_gather | solution.py:23
  141.9 21.5 %multiply_convert_fusion = (bf16[2,16,64,512]{3,2,1,0:T(8,128)(2,1)}, bf16[2,16,64,512]{3,2,1,0:T(8,128)(2,1)}, bf16[2,16,64]{2,1,0:T(8,128)(2,1)S(1)}) fusion(f32[2,16,64]{2,1,0:T(8,128)S(1)} %copy.37, f32[1024,2,512]{2,1,0:T(2,128)} %convert_element_type.97, f32[1024,2,512]{2,1,0:T(2,128)} %convert_element_type.96, f32[2,16,64,512]{3,2,1,0:T(8,128)} %bitcast.49, ...), kind=kOutput, calls=%fused_computation.12 | convolution fusion | flops 9417521152 | bytes 43020288 | tf_op jit(solution)/shard_map/lbcd,lfd->lbcf/dot_general | solution.py:33
  163.4 0.0 copy-start.4
  163.4 16.4 %fusion.6 = f32[2,16,64,3584]{3,2,0,1:T(8,128)} fusion(bf16[2,3584,512]{2,1,0:T(8,128)(2,1)} %param.14, bf16[2,16,64,512]{3,2,1,0:T(8,128)(2,1)} %get-tuple-element.2), kind=kOutput, calls=%fused_computation.7 | convolution fusion | flops 7516192768 | bytes 38797312 | tf_op jit(solution)/shard_map/lbcf,ldf->lbcd/dot_general | solution.py:63
  179.8 0.0 copy-done.4
  179.8 16.6 %fusion.8 = f32[2,16,64,3584]{3,2,0,1:T(8,128)} fusion(bf16[2,3584,512]{2,1,0:T(8,128)(2,1)} %param.13, bf16[2,16,64,512]{3,2,1,0:T(8,128)(2,1)S(1)} %copy-done.4), kind=kOutput, calls=%fused_computation.9 | convolution fusion | flops 7516192768 | bytes 38797312 | tf_op jit(solution)/shard_map/lbcf,ldf->lbcd/dot_general | solution.py:60
  196.4 25.0 %bitcast_convert_fusion = bf16[16,128,3584]{2,1,0:T(8,128)(2,1)} fusion(f32[2,16,64,3584]{3,2,0,1:T(8,128)} %fusion.8, f32[2,16,64,3584]{3,2,0,1:T(8,128)} %fusion.6, f32[16,2,128]{2,1,0:T(2,128)S(1)} %copy.36), kind=kOutput, calls=%fused_computation | convolution fusion | flops 1901330432 | bytes 73416704 | tf_op jit(solution)/shard_map/blct,lbcd->btd/dot_general | solution.py:66
  221.4 0.0 reduce-scatter.3.cloned.1.call-update
  221.4 0.0 reduce-scatter.5.cloned.1.call-start
  221.5 22.3 %reduce-scatter.3.cloned.1.call-done = bf16[2048,1792]{1,0:T(8,128)(2,1)} async-done(((bf16[2048,3584]{1,0:T(8,128)(2,1)}), bf16[2048,1792]{1,0:T(8,128)(2,1)}) %reduce-scatter.3.cloned.1.call-update) | async-done | bytes 7340048 | tf_op jit(solution)/shard_map/reduce_scatter | solution.py:70
  243.8 0.0 reduce-scatter.5.cloned.1.call-update
  243.8 0.3 fusion.15
  244.1 2.5 psum.7
  246.6 11.8 %all_to_all.10 = bf16[16,2,128]{2,1,0:T(2,128)(2,1)S(1)} all-to-all(bf16[16,2,128]{2,1,0:T(2,128)(2,1)S(1)} %psum.7), channel_id=1, replica_groups=mesh['expert'=16,'etp'=2] {'expert'}, dimensions={0} | all-to-all | bytes 16384 | tf_op jit(solution)/shard_map/all_to_all | solution.py:55
  258.4 0.6 select_reduce_fusion.1
  259.1 147.7 %reduce-scatter.5.cloned.1.call-done = bf16[128,1792]{1,0:T(8,128)(2,1)} async-done(((bf16[2048,1792]{1,0:T(8,128)(2,1)}), bf16[128,1792]{1,0:T(8,128)(2,1)}) %reduce-scatter.5.cloned.1.call-update) | async-done | bytes 458768 | tf_op jit(solution)/shard_map/reduce_scatter | solution.py:71
  (8 shorter events, 0.1 us)
Async XLA Ops:
  7.2 106.9 %copy-start.3 = (bf16[128,8]{0,1:T(8,128)(2,1)S(1)}, bf16[128,8]{0,1:T(8,128)(2,1)}, u32[]{:S(2)}) copy-start(bf16[128,8]{0,1:T(8,128)(2,1)} %param.9) | copy-start | bytes 6148
  7.2 106.9 %copy-start.2 = (s32[128,8]{0,1:T(8,128)S(1)}, s32[128,8]{0,1:T(8,128)}, u32[]{:S(2)}) copy-start(s32[128,8]{0,1:T(8,128)} %param.10) | copy-start | bytes 12292
  7.2 112.6 %copy-start = (bf16[1024,2,512]{2,1,0:T(2,128)(2,1)S(1)}, bf16[1024,2,512]{2,1,0:T(2,128)(2,1)}, u32[]{:S(2)}) copy-start(bf16[1024,2,512]{2,1,0:T(2,128)(2,1)} %param.11) | copy-start | bytes 6291460
  7.2 106.8 %all-gather.3.cloned.1.call-start = ((), (), s32[]{:S(2)}) async-start(), calls=%async_computation.4 | async-start | bytes 7798784 | tf_op jit(solution)/shard_map/all_gather | solution.py:22
  7.9 134.0 %all-gather.5.cloned.1.call-start = ((), (), s32[]{:S(2)}) async-start(), calls=%async_computation.5 | async-start | bytes 22020096 | tf_op jit(solution)/shard_map/all_gather | solution.py:23
  114.7 19.2 %all-to-all-start = ((bf16[16,2,128]{2,1,0:T(2,128)(2,1)}), bf16[16,2,128]{2,1,0:T(2,128)(2,1)S(1)}, u32[]{:S(2)}, u32[]{:S(2)}) async-start(bf16[16,2,128]{2,1,0:T(2,128)(2,1)} %bitcast.1), calls=%async_computation | async-start | bytes 16384 | tf_op jit(solution)/shard_map/all_to_all | solution.py:19
  119.7 124.0 %reduce-scatter.3.cloned.1.call-start = ((), (), s32[]{:S(2)}) async-start(), calls=%async_computation.6 | async-start | bytes 22020096 | tf_op jit(solution)/shard_map/reduce_scatter | solution.py:70
  122.9 4.2 %copy-start.1 = (bf16[1024,2,512]{2,1,0:T(2,128)(2,1)S(1)}, bf16[1024,2,512]{2,1,0:T(2,128)(2,1)}, u32[]{:S(2)}) copy-start(bf16[1024,2,512]{2,1,0:T(2,128)(2,1)} %param.12) | copy-start | bytes 6291460
  163.4 16.4 %copy-start.4 = (bf16[2,16,64,512]{3,2,1,0:T(8,128)(2,1)S(1)}, bf16[2,16,64,512]{3,2,1,0:T(8,128)(2,1)}, u32[]{:S(2)}) copy-start(bf16[2,16,64,512]{3,2,1,0:T(8,128)(2,1)} %get-tuple-element.3) | copy-start | bytes 6291460
  221.4 185.3 %reduce-scatter.5.cloned.1.call-start = ((), (), s32[]{:S(2)}) async-start(), calls=%async_computation.7 | async-start | bytes 7798784 | tf_op jit(solution)/shard_map/reduce_scatter | solution.py:71
Sparse Core Ops, SparseCore 0:
  10.7 103.3 all-gather.2
  115.6 26.2 all-gather.4
  221.5 22.2 reduce-scatter.2
  246.5 160.1 reduce-scatter.4
where the time goes:
time: 414 us; the launch traced here: 413 us
  waiting for transfers between devices  284 us (69%)
  matrix products  79.8 us (19%)
  blocking collectives  14.3 us (3%)
  between operations  13.9 us (3%)
  other arithmetic  10.5 us (3%)
  local copies, waits for them, and re-layouts  6.03 us (1%)
  starting transfers between devices  5.19 us (1%)
    reduce_scatter x1, waiting for transfers between devices, on_device(): lax.psum_scatter(partial, 'expert', scatter_dimension=0, tiled=True)  148 us
    all_gather x1, waiting for transfers between devices, on_device(): rows = lax.all_gather(grad_out, 'expert', axis=0, tiled=True)  106 us
    dot_general x1, matrix products, on_device(): jnp.einsum('blct,lbcd->btd', select, partial.astype(jnp.bfloat16), prefer...  25 us
    reduce_scatter x1, waiting for transfers between devices, on_device(): partial = lax.psum_scatter(partial, 'etp', scatter_dimension=1, tiled=True)  22.3 us
    dot_general x1, matrix products, on_device(): jnp.einsum('lbcd,lfd->lbcf', slot_rows, down_weight, preferred_element_ty...  21.5 us
    dot_general x1, matrix products, on_device(): jnp.einsum('lbcf,ldf->lbcd', grad_gate, gate_weight, preferred_element_ty...  16.6 us
    dot_general x1, matrix products, on_device(): jnp.einsum('lbcf,ldf->lbcd', grad_up, up_weight, preferred_element_type=j...  16.4 us
    all_to_all x1, blocking collectives, on_device(): lax.all_to_all(weight_tok, 'expert', split_axis=0, concat_axis=0, tiled=T...  11.8 us
  transfers between devices with their start and end apart: 5, of which 4 were waited for; matrix products, arithmetic and copies ran while one was open for 4% of the time, Pallas kernels for 0%

commit v1 on v0

--- a/solution.py
+++ b/solution.py
@@ -19,7 +19,8 @@
     weights = lax.all_to_all(
         weights.transpose(1, 2, 0), "expert", split_axis=0, concat_axis=0, tiled=True
     )
-    rows = lax.all_gather(grad_out, "expert", axis=0, tiled=True)
+    outgoing = jnp.stack([grad_out] * lax.axis_size("expert"))
+    rows = jnp.concatenate(lax.all_to_all(outgoing, "expert", 0, 0), axis=0)
     rows = lax.all_gather(rows, "etp", axis=1, tiled=True)
     rows = rows.reshape(groups, tokens, -1)
     named = (weights > 0).astype(jnp.float32)

time: 414 us -> 474 us (1.14)
  blocking collectives: 14.3 us -> 181 us
  waiting for transfers between devices: 284 us -> 175 us
    all_to_all x0 -> x1, blocking collectives: none -> 167 us  [on_device(): rows = jnp.concatenate(lax.all_to_all(outgoing, 'expert', 0, 0), axis=0)]
    all_gather x1 -> x0, waiting for transfers between devices: 106 us -> none  [on_device(): rows = lax.all_gather(grad_out, 'expert', axis=0, tiled=True)]
  transfers between devices with their start and end apart: 5 -> 4, of which waited for: 4 -> 3; matrix products, arithmetic and copies ran while one was open for 4% -> 3% of each run, Pallas kernels for 0% -> 0%
where the time goes in v1:
time: 474 us
  blocking collectives  181 us (38%)
  waiting for transfers between devices  175 us (37%)
  matrix products  79.8 us (17%)
  between operations  13.8 us (3%)
  other arithmetic  9.78 us (2%)
  local copies, waits for them, and re-layouts  8.92 us (2%)
  starting transfers between devices  5.58 us (1%)
    all_to_all x1, blocking collectives, on_device(): rows = jnp.concatenate(lax.all_to_all(outgoing, 'expert', 0, 0), axis=0)  167 us
    reduce_scatter x1, waiting for transfers between devices, on_device(): lax.psum_scatter(partial, 'expert', scatter_dimension=0, tiled=True)  148 us
    dot_general x1, matrix products, on_device(): jnp.einsum('blct,lbcd->btd', select, partial.astype(jnp.bfloat16), prefer...  25 us
    reduce_scatter x1, waiting for transfers between devices, on_device(): partial = lax.psum_scatter(partial, 'etp', scatter_dimension=1, tiled=True)  22.3 us
    dot_general x1, matrix products, on_device(): jnp.einsum('lbcd,lfd->lbcf', slot_rows, down_weight, preferred_element_ty...  21.5 us
    dot_general x1, matrix products, on_device(): jnp.einsum('lbcf,ldf->lbcd', grad_gate, gate_weight, preferred_element_ty...  16.6 us
    dot_general x1, matrix products, on_device(): jnp.einsum('lbcf,ldf->lbcd', grad_up, up_weight, preferred_element_type=j...  16.4 us
    all_to_all x1, blocking collectives, on_device(): lax.all_to_all(weight_tok, 'expert', split_axis=0, concat_axis=0, tiled=T...  11.8 us
  transfers between devices with their start and end apart: 4, of which 3 were waited for; matrix products, arithmetic and copies ran while one was open for 3% of the time, Pallas kernels for 0%

profile of v1, /device:TPU:10, one launch (start us, length us, event | category | flops | bytes accessed | tf_op | source)
XLA Modules:
  0.0 474.1 jit_solution(7451369004410705761)
XLA Ops:
  7.2 0.0 all-gather.2.cloned.1.call-start
  7.2 1.7 stack.2
  8.9 166.7 %all_to_all.15 = bf16[16,128,1792]{2,1,0:T(8,128)(2,1)} all-to-all(bf16[16,128,1792]{2,1,0:T(8,128)(2,1)S(1)} %stack.2), channel_id=1, replica_groups=mesh['expert'=16,'etp'=2] {'expert'}, dimensions={0} | all-to-all | bytes 14680064 | tf_op jit(solution)/shard_map/all_to_all | solution.py:23
  175.7 0.0 copy-start.3
  175.7 0.0 copy-start.2
  175.7 0.0 copy-start
  175.7 0.0 all-gather.2.cloned.1.call-update
  175.7 0.7 copy-done.3
  176.4 0.0 copy-done.2
  176.4 0.6 select_reduce_fusion.2
  177.0 5.5 %all-to-all-start = ((bf16[16,2,128]{2,1,0:T(2,128)(2,1)}), bf16[16,2,128]{2,1,0:T(2,128)(2,1)S(1)}, u32[]{:S(2)}, u32[]{:S(2)}) async-start(bf16[16,2,128]{2,1,0:T(2,128)(2,1)} %bitcast.1), calls=%async_computation | async-start | bytes 16384 | tf_op jit(solution)/shard_map/all_to_all | solution.py:19
  182.5 0.0 reduce-scatter.3.cloned.1.call-start
  182.5 0.0 copy-done
  182.5 3.6 copy.40
  186.1 0.0 copy-start.1
  186.1 3.8 convert_element_type.97
  189.9 0.0 copy-done.1
  189.9 2.9 copy.39
  192.9 3.5 convert_element_type.96
  196.4 0.0 all-to-all-done
  196.4 0.8 reduce_window_sum.11
  197.2 0.4 select_reduce_fusion
  197.6 5.0 %all-gather.2.cloned.1.call-done = bf16[2048,3584]{1,0:T(8,128)(2,1)} async-done(((bf16[2048,1792]{1,0:T(8,128)(2,1)}), bf16[2048,3584]{1,0:T(8,128)(2,1)}) %all-gather.2.cloned.1.call-update) | async-done | bytes 14680080 | tf_op jit(solution)/shard_map/all_gather | solution.py:24
  202.6 21.5 %multiply_convert_fusion = (bf16[2,16,64,512]{3,2,1,0:T(8,128)(2,1)}, bf16[2,16,64,512]{3,2,1,0:T(8,128)(2,1)}, bf16[2,16,64]{2,1,0:T(8,128)(2,1)S(1)}) fusion(f32[2,16,64]{2,1,0:T(8,128)S(1)} %copy.37, f32[1024,2,512]{2,1,0:T(2,128)} %convert_element_type.97, f32[1024,2,512]{2,1,0:T(2,128)} %convert_element_type.96, f32[2,16,64,512]{3,2,1,0:T(8,128)} %bitcast.51, ...), kind=kOutput, calls=%fused_computation.12 | convolution fusion | flops 9417521152 | bytes 43020288 | tf_op jit(solution)/shard_map/lbcd,lfd->lbcf/dot_general | solution.py:34
  224.1 0.0 copy-start.4
  224.1 16.4 %fusion.6 = f32[2,16,64,3584]{3,2,0,1:T(8,128)} fusion(bf16[2,3584,512]{2,1,0:T(8,128)(2,1)} %param.14, bf16[2,16,64,512]{3,2,1,0:T(8,128)(2,1)} %get-tuple-element.2), kind=kOutput, calls=%fused_computation.7 | convolution fusion | flops 7516192768 | bytes 38797312 | tf_op jit(solution)/shard_map/lbcf,ldf->lbcd/dot_general | solution.py:64
  240.4 0.0 copy-done.4
  240.4 16.6 %fusion.8 = f32[2,16,64,3584]{3,2,0,1:T(8,128)} fusion(bf16[2,3584,512]{2,1,0:T(8,128)(2,1)} %param.13, bf16[2,16,64,512]{3,2,1,0:T(8,128)(2,1)S(1)} %copy-done.4), kind=kOutput, calls=%fused_computation.9 | convolution fusion | flops 7516192768 | bytes 38797312 | tf_op jit(solution)/shard_map/lbcf,ldf->lbcd/dot_general | solution.py:61
  257.0 25.0 %bitcast_convert_fusion = bf16[16,128,3584]{2,1,0:T(8,128)(2,1)} fusion(f32[2,16,64,3584]{3,2,0,1:T(8,128)} %fusion.8, f32[2,16,64,3584]{3,2,0,1:T(8,128)} %fusion.6, f32[16,2,128]{2,1,0:T(2,128)S(1)} %copy.36), kind=kOutput, calls=%fused_computation | convolution fusion | flops 1901330432 | bytes 73416704 | tf_op jit(solution)/shard_map/blct,lbcd->btd/dot_general | solution.py:67
  282.1 0.0 reduce-scatter.3.cloned.1.call-update
  282.1 0.0 reduce-scatter.5.cloned.1.call-start
  282.1 22.3 %reduce-scatter.3.cloned.1.call-done = bf16[2048,1792]{1,0:T(8,128)(2,1)} async-done(((bf16[2048,3584]{1,0:T(8,128)(2,1)}), bf16[2048,1792]{1,0:T(8,128)(2,1)}) %reduce-scatter.3.cloned.1.call-update) | async-done | bytes 7340048 | tf_op jit(solution)/shard_map/reduce_scatter | solution.py:71
  304.5 0.0 reduce-scatter.5.cloned.1.call-update
  304.5 0.3 fusion.15
  304.8 2.5 psum.7
  307.3 11.8 %all_to_all.16 = bf16[16,2,128]{2,1,0:T(2,128)(2,1)S(1)} all-to-all(bf16[16,2,128]{2,1,0:T(2,128)(2,1)S(1)} %psum.7), channel_id=1, replica_groups=mesh['expert'=16,'etp'=2] {'expert'}, dimensions={0} | all-to-all | bytes 16384 | tf_op jit(solution)/shard_map/all_to_all | solution.py:56
  319.1 0.6 select_reduce_fusion.1
  319.7 147.8 %reduce-scatter.5.cloned.1.call-done = bf16[128,1792]{1,0:T(8,128)(2,1)} async-done(((bf16[2048,1792]{1,0:T(8,128)(2,1)}), bf16[128,1792]{1,0:T(8,128)(2,1)}) %reduce-scatter.5.cloned.1.call-update) | async-done | bytes 458768 | tf_op jit(solution)/shard_map/reduce_scatter | solution.py:72
  (8 shorter events, 0.1 us)
Async XLA Ops:
  7.2 195.4 %all-gather.2.cloned.1.call-start = ((), (), s32[]{:S(2)}) async-start(), calls=%async_computation.5 | async-start | bytes 22020096 | tf_op jit(solution)/shard_map/all_gather | solution.py:24
  175.7 0.7 copy-start.3
  175.7 0.7 copy-start.2
  175.7 6.8 %copy-start = (bf16[1024,2,512]{2,1,0:T(2,128)(2,1)S(1)}, bf16[1024,2,512]{2,1,0:T(2,128)(2,1)}, u32[]{:S(2)}) copy-start(bf16[1024,2,512]{2,1,0:T(2,128)(2,1)} %param.11) | copy-start | bytes 6291460
  177.0 19.4 %all-to-all-start = ((bf16[16,2,128]{2,1,0:T(2,128)(2,1)}), bf16[16,2,128]{2,1,0:T(2,128)(2,1)S(1)}, u32[]{:S(2)}, u32[]{:S(2)}) async-start(bf16[16,2,128]{2,1,0:T(2,128)(2,1)} %bitcast.1), calls=%async_computation | async-start | bytes 16384 | tf_op jit(solution)/shard_map/all_to_all | solution.py:19
  182.5 122.0 %reduce-scatter.3.cloned.1.call-start = ((), (), s32[]{:S(2)}) async-start(), calls=%async_computation.6 | async-start | bytes 22020096 | tf_op jit(solution)/shard_map/reduce_scatter | solution.py:71
  186.1 3.9 copy-start.1
  224.1 16.4 %copy-start.4 = (bf16[2,16,64,512]{3,2,1,0:T(8,128)(2,1)S(1)}, bf16[2,16,64,512]{3,2,1,0:T(8,128)(2,1)}, u32[]{:S(2)}) copy-start(bf16[2,16,64,512]{3,2,1,0:T(8,128)(2,1)} %get-tuple-element.3) | copy-start | bytes 6291460
  282.1 185.5 %reduce-scatter.5.cloned.1.call-start = ((), (), s32[]{:S(2)}) async-start(), calls=%async_computation.7 | async-start | bytes 7798784 | tf_op jit(solution)/shard_map/reduce_scatter | solution.py:72
Sparse Core Ops, SparseCore 0:
  175.8 26.6 all-gather.1
  282.2 22.2 reduce-scatter.2
  307.3 160.1 reduce-scatter.4
